TPU v7x, 32 devices: a whole 2x2x4 slice. The times are simulated.
32 devices in a mesh: dp: 4 (over x, core), expert: 8 (over z, y).
Axes of the slice: x: 2, y: 2, z: 4, core: 2. Of those that a mesh axis runs over, the one named last changes fastest.
Arguments:
- tokens: bfloat16 [16384, 768], P(('dp', 'expert')), may hold values from -6 to 6
- cotangent: bfloat16 [16384, 768], P(('dp', 'expert')), may hold values from -6 to 6
- chosen: int32 [16384, 2], P(('dp', 'expert')), may hold values from 0 to 9, all different within a row; in each aligned block of 512 rows (0 to 511, 512 to 1023, ...) at most 128 rows name the same one
- gates: float32 [16384, 2], P(('dp', 'expert')), may hold values from 0.2 to 0.8
- lengths: int32 [32, 8], P(('dp', 'expert')), may hold values from 1 to 256, 512 in all within a row
- keep_mask: int32 [16384], P(('dp', 'expert')), may hold values 0 or 1
- gain1: float32 [768], replicated, may hold values from 0.5 to 1.5
- w_qkv: bfloat16 [768, 2304], replicated, may hold values from -0.21875 to 0.21875
- w_o: bfloat16 [768, 768], replicated, may hold values from -0.875 to 0.875
- gain2: float32 [768], replicated, may hold values from 0.5 to 1.5
- frozen_in: bfloat16 [2, 3072, 768], replicated, may hold values from -0.21875 to 0.21875
- frozen_out: bfloat16 [2, 3072, 768], replicated, may hold values from -0.109375 to 0.109375
- w_in: bfloat16 [8, 3072, 768], P('expert', 'dp'), may hold values from -0.21875 to 0.21875
- w_out: bfloat16 [8, 3072, 768], P('expert', 'dp'), may hold values from -0.109375 to 0.109375
Outputs:
- output: bfloat16 [16384, 768], P(('dp', 'expert'))
- d_tokens: bfloat16 [16384, 768], P(('dp', 'expert'))
- d_gain1: float32 [768], replicated
- d_w_qkv: float32 [768, 2304], replicated
- d_w_o: float32 [768, 768], replicated
- d_gain2: float32 [768], replicated
- d_w_in: float32 [8, 3072, 768], P('expert', 'dp')
- d_w_out: float32 [8, 3072, 768], P('expert', 'dp')
- counts: float32 [10], replicated
Inputs may be any that keep to these rules, and one draw needn't show every extreme that they name: `chosen`: each token names two different experts; among the 512 tokens of one device no expert is named more than 128 times, a bound that some block reaches. The 8 lengths of a device sum to 512; the longest is exactly 256.
All inputs are finite; a program needn't handle non-finite values. No bound on the sum of `keep_mask` on one device may be relied on, other than what follows from the above.
Results may differ from a plain program's by a relative error of at most 0.012.
Values may be sent and summed in bfloat16 or wider, within the bound.
A program may use at most 256 MiB of HBM per device.

v0:
```python
import jax
import jax.numpy as jnp
from jax import lax
from jax.sharding import PartitionSpec as P

HEADS = 12
HEAD_DIM = 64
FROZEN = 2


def layer_norm(values_in, gain_vec):
    row_mean = jnp.mean(values_in, axis=-1, keepdims=True)
    centred = values_in - row_mean
    variance = jnp.mean(centred * centred, axis=-1, keepdims=True)
    return centred * lax.rsqrt(variance + 1e-05) * gain_vec


def expert_forward(rows_low, up_weights, down_weights):
    hidden = jnp.einsum("gcd,gfd->gcf", rows_low, up_weights, preferred_element_type=jnp.float32)
    active = jax.nn.gelu(hidden).astype(jnp.bfloat16)
    result_rows = jnp.einsum(
        "gcf,gfd->gcd", active, down_weights, preferred_element_type=jnp.float32
    ).astype(jnp.bfloat16)
    return (result_rows, hidden)


def expert_backward(result_grad, hidden, up_weights, down_weights):
    active_grad = jnp.einsum(
        "gcd,gfd->gcf", result_grad, down_weights, preferred_element_type=jnp.float32
    )
    active, gelu_back = jax.vjp(jax.nn.gelu, hidden)
    hidden_grad = gelu_back(active_grad)[0].astype(jnp.bfloat16)
    input_grad = jnp.einsum(
        "gcf,gfd->gcd", hidden_grad, up_weights, preferred_element_type=jnp.float32
    ).astype(jnp.bfloat16)
    return (input_grad, hidden_grad, active.astype(jnp.bfloat16))


def block_scores(query_part, key_heads, allowed):
    scores = (
        jnp.einsum("qhd,khd->hqk", query_part, key_heads, preferred_element_type=jnp.float32)
        * 0.125
    )
    return jnp.where(allowed[None], scores, -1e30)


def body(
    tokens,
    cotangent,
    chosen,
    gates,
    lengths,
    keep_mask,
    gain1,
    w_qkv,
    w_o,
    gain2,
    frozen_in,
    frozen_out,
    w_in,
    w_out,
):
    row_count = tokens.shape[0]
    feat_width = tokens.shape[1]
    owners = lax.axis_size("expert")
    kind_count = FROZEN + owners
    slot_count = (2 * row_count * 5 // (4 * kind_count) + 7) // 8 * 8
    block_rows = min(512, row_count)
    weights_in, weights_out = (
        lax.all_gather(w_in, "dp", axis=1, tiled=True),
        lax.all_gather(w_out, "dp", axis=1, tiled=True),
    )
    tokens_full = tokens.astype(jnp.float32)
    normed_one, norm_one_back = jax.vjp(layer_norm, tokens_full, gain1)
    normed_one_low = normed_one.astype(jnp.bfloat16)
    projected = jnp.dot(normed_one_low, w_qkv, preferred_element_type=jnp.float32).astype(
        jnp.bfloat16
    )
    queries = projected[:, :feat_width].reshape(row_count, HEADS, HEAD_DIM)
    key_heads = projected[:, feat_width : 2 * feat_width].reshape(row_count, HEADS, HEAD_DIM)
    value_heads = projected[:, 2 * feat_width :].reshape(row_count, HEADS, HEAD_DIM)
    places = jnp.arange(row_count, dtype=jnp.int32)
    doc_ends = jnp.cumsum(lengths[0])
    documents = jnp.sum((places[:, None] >= doc_ends[None, :]).astype(jnp.int32), axis=1)

    def permitted():
        return (
            (documents[:, None] == documents[None, :])
            & (places[None, :] <= places[:, None])
            & ((keep_mask[None, :] > 0) | (places[None, :] == places[:, None]))
        )

    scores = block_scores(queries, key_heads, permitted())
    peak_score = jnp.max(scores, axis=-1, keepdims=True)
    exp_scores = jnp.exp(scores - peak_score)
    exp_total = jnp.sum(exp_scores, axis=-1, keepdims=True)
    probs_low = (exp_scores / exp_total).astype(jnp.bfloat16)
    block_out = jnp.einsum(
        "hqk,khd->qhd", probs_low, value_heads, preferred_element_type=jnp.float32
    )
    out_blocks = block_out.reshape(block_rows, feat_width).astype(jnp.bfloat16)
    lse_blocks = [peak_score + jnp.log(exp_total)]
    mixed_rows = tokens_full + jnp.dot(out_blocks, w_o, preferred_element_type=jnp.float32)
    normed_two, norm_two_back = jax.vjp(layer_norm, mixed_rows, gain2)
    normed_two_low = normed_two.astype(jnp.bfloat16)
    flat_ids = chosen.reshape(-1)
    one_hot = (flat_ids[:, None] == jnp.arange(kind_count, dtype=jnp.int32)[None, :]).astype(
        jnp.int32
    )
    slot_ranks = jnp.sum(jnp.cumsum(one_hot, axis=0) * one_hot, axis=1) - 1
    positions = flat_ids * slot_count + slot_ranks
    buffer_rows = (
        jnp.zeros((kind_count * slot_count, feat_width), jnp.bfloat16)
        .at[positions]
        .set(jnp.repeat(normed_two_low, 2, axis=0))
    )
    local_rows = buffer_rows[: FROZEN * slot_count].reshape(FROZEN, slot_count, feat_width)
    routed_rows = buffer_rows[FROZEN * slot_count :].reshape(owners, slot_count, feat_width)
    arrived_rows = lax.all_to_all(routed_rows, "expert", split_axis=0, concat_axis=0, tiled=True)
    result_rows, _ = expert_forward(
        arrived_rows.reshape(1, -1, feat_width), weights_in, weights_out
    )
    served = result_rows.reshape(arrived_rows.shape)
    frozen_result, frozen_hidden = expert_forward(local_rows, frozen_in, frozen_out)
    returned = lax.all_to_all(served, "expert", split_axis=0, concat_axis=0, tiled=True)
    results = jnp.concatenate(
        [frozen_result.reshape(-1, feat_width), returned.reshape(-1, feat_width)], axis=0
    )
    picked = results[positions].astype(jnp.float32).reshape(row_count, 2, feat_width)
    output = mixed_rows + jnp.sum(picked * gates[:, :, None], axis=1)
    grad_out = cotangent.astype(jnp.float32)
    weighted = (jnp.repeat(grad_out, 2, axis=0) * gates.reshape(-1, 1)).astype(jnp.bfloat16)
    grad_buffer = (
        jnp.zeros((kind_count * slot_count, feat_width), jnp.bfloat16).at[positions].set(weighted)
    )
    frozen_grad_rows = grad_buffer[: FROZEN * slot_count].reshape(FROZEN, slot_count, feat_width)
    routed_grad = grad_buffer[FROZEN * slot_count :].reshape(owners, slot_count, feat_width)
    arrived_grad = lax.all_to_all(routed_grad, "expert", split_axis=0, concat_axis=0, tiled=True)
    flat_rows = arrived_rows.reshape(1, -1, feat_width)
    flat_grad = arrived_grad.reshape(1, -1, feat_width)
    hidden_all = jnp.einsum(
        "gcd,gfd->gcf", flat_rows, weights_in, preferred_element_type=jnp.float32
    )
    row_input_grad, hidden_grad, active = expert_backward(
        flat_grad, hidden_all, weights_in, weights_out
    )
    sent_back = lax.all_to_all(
        row_input_grad.reshape(owners, slot_count, feat_width),
        "expert",
        split_axis=0,
        concat_axis=0,
        tiled=True,
    )
    frozen_input_grad, _, _ = expert_backward(
        frozen_grad_rows, frozen_hidden, frozen_in, frozen_out
    )
    hidden_rows = hidden_grad[0]
    active_rows = active[0]
    input_rows = flat_rows[0]
    output_rows = flat_grad[0]
    term_in = lax.dot_general(
        hidden_rows, input_rows, (((0,), (0,)), ((), ())), preferred_element_type=jnp.float32
    )
    term_out = lax.dot_general(
        active_rows, output_rows, (((0,), (0,)), ((), ())), preferred_element_type=jnp.float32
    )
    summed = lax.psum_scatter(
        jnp.concatenate([term_in, term_out], axis=1), "dp", scatter_dimension=0, tiled=True
    )
    d_w_in = summed[:, :feat_width][None]
    d_w_out = summed[:, feat_width:][None]
    row_grads = jnp.concatenate(
        [frozen_input_grad.reshape(-1, feat_width), sent_back.reshape(-1, feat_width)], axis=0
    )
    normed_two_grad = jnp.sum(
        row_grads[positions].astype(jnp.float32).reshape(row_count, 2, feat_width), axis=1
    )
    mixed_part, gain2_grad = norm_two_back(normed_two_grad)
    mixed_grad = grad_out + mixed_part
    branch_grad = mixed_grad.astype(jnp.bfloat16)
    w_o_grad = lax.dot_general(
        out_blocks, branch_grad, (((0,), (0,)), ((), ())), preferred_element_type=jnp.float32
    )
    attended_grad = lax.dot_general(
        branch_grad, w_o, (((1,), (1,)), ((), ())), preferred_element_type=jnp.float32
    ).astype(jnp.bfloat16)
    attended_heads = attended_grad.reshape(row_count, HEADS, HEAD_DIM)
    key_grad = jnp.zeros((row_count, HEADS, HEAD_DIM), jnp.float32)
    value_grad = jnp.zeros((row_count, HEADS, HEAD_DIM), jnp.float32)
    query_grads = []
    for block_index, row_start in enumerate(range(0, row_count, block_rows)):
        scores = block_scores(queries, key_heads, permitted())
        probs_full = jnp.exp(scores - lse_blocks[block_index])
        probs_low = probs_full.astype(jnp.bfloat16)
        prob_grad = jnp.einsum(
            "qhd,khd->hqk", attended_heads, value_heads, preferred_element_type=jnp.float32
        )
        row_delta = jnp.sum(probs_full * prob_grad, axis=-1, keepdims=True)
        score_grad = (probs_full * (prob_grad - row_delta)).astype(jnp.bfloat16)
        query_grads.append(
            jnp.einsum("hqk,khd->qhd", score_grad, key_heads, preferred_element_type=jnp.float32)
            * 0.125
        )
        key_grad = (
            jnp.einsum("hqk,qhd->khd", score_grad, queries, preferred_element_type=jnp.float32)
            * 0.125
        )
        value_grad = jnp.einsum(
            "hqk,qhd->khd", probs_low, attended_heads, preferred_element_type=jnp.float32
        )
    projected_grad = jnp.concatenate(
        [
            query_grads[0].reshape(row_count, feat_width),
            key_grad.reshape(row_count, feat_width),
            value_grad.reshape(row_count, feat_width),
        ],
        axis=1,
    ).astype(jnp.bfloat16)
    w_qkv_grad = lax.dot_general(
        normed_one_low, projected_grad, (((0,), (0,)), ((), ())), preferred_element_type=jnp.float32
    )
    normed_one_grad = lax.dot_general(
        projected_grad, w_qkv, (((1,), (1,)), ((), ())), preferred_element_type=jnp.float32
    )
    tokens_part, gain1_grad = norm_one_back(normed_one_grad)
    tokens_grad = (mixed_grad + tokens_part).astype(jnp.bfloat16)
    local_counts = jnp.sum(one_hot, axis=0).astype(jnp.float32)
    gain1_sum, w_qkv_sum, w_o_sum, gain2_sum, counts = lax.psum(
        (gain1_grad, w_qkv_grad, w_o_grad, gain2_grad, local_counts), ("dp", "expert")
    )
    return (
        output.astype(jnp.bfloat16),
        tokens_grad,
        gain1_sum,
        w_qkv_sum,
        w_o_sum,
        gain2_sum,
        d_w_in,
        d_w_out,
        counts,
    )


def solution(mesh):
    placed = (
        P(("dp", "expert"), None),
        P(("dp", "expert"), None),
        P(("dp", "expert"), None),
        P(("dp", "expert"), None),
        P(("dp", "expert"), None),
        P(("dp", "expert")),
        P(),
        P(),
        P(),
        P(),
        P(),
        P(),
        P("expert", "dp", None),
        P("expert", "dp", None),
    )
    return jax.shard_map(
        body,
        mesh=mesh,
        in_specs=placed,
        out_specs=(
            P(("dp", "expert"), None),
            P(("dp", "expert"), None),
            P(),
            P(),
            P(),
            P(),
            P("expert", "dp", None),
            P("expert", "dp", None),
            P(),
        ),
        check_vma=False,
    )
```

profile of v0, /device:TPU:0, one launch (start us, length us, event | category | flops | bytes accessed | tf_op | source)
XLA Modules:
  0.0 601.5 jit_solution(12574793378495375460)
XLA Ops:
  14.4 6.2 %reduce-window.19 = s32[10,8,128]{2,1,0:T(8,128)} reduce-window(s32[10,8,128]{2,1,0:T(8,128)} %fusion.76, s32[]{:T(128)} %constant.21.clone.1), window={size=1x1x128 pad=0_0x0_0x127_0}, to_apply=%region_6.7 | reduce-window | flops 1300480 | bytes 81924 | tf_op jit(solution)/shard_map/reduce-window.1
  27.1 4.7 convolution_convert_fusion
  37.2 3.1 fusion.100
  47.6 3.5 fusion.21
  51.1 3.7 fusion.7
  55.7 5.1 fusion.59
  65.7 4.6 reshape.407
  71.9 7.2 %scatter_custom_fusion = bf16[1280,768]{1,0:T(8,128)(2,1)} fusion(s32[1024]{0:T(1024)S(1)} %bitcast.116, bf16[1024,768]{1,0:T(8,128)(2,1)} %reshape.407, bf16[]{:T(256)} %constant.25.clone.1), kind=kCustom, calls=%fused_computation.98 | custom fusion | bytes 1966592 | tf_op jit(solution)/shard_map/scatter | solution.py:115
  81.8 7.3 %all-to-all-start = ((bf16[8,128,768]{2,1,0:T(8,128)(2,1)}), bf16[8,128,768]{2,1,0:T(8,128)(2,1)}, u32[]{:S(2)}, u32[]{:S(2)}) async-start(bf16[8,128,768]{2,1,0:T(8,128)(2,1)} %bitcast.96), calls=%async_computation | async-start | bytes 3145728 | tf_op jit(solution)/shard_map/all_to_all | solution.py:119
  91.8 3.6 broadcast_in_dim.35
  95.4 5.4 reshape.374
  100.8 8.1 %scatter_custom_fusion.1 = bf16[1280,768]{1,0:T(8,128)(2,1)} fusion(s32[1024]{0:T(1024)S(1)} %bitcast.117, f32[1024,768]{1,0:T(8,128)} %reshape.374, f32[1024]{0:T(1024)S(1)} %mul.298, bf16[]{:T(256)} %constant.25.clone.1), kind=kCustom, calls=%fused_computation.71 | custom fusion | flops 1572864 | bytes 5115906 | tf_op jit(solution)/shard_map/scatter | solution.py:134
  111.5 14.8 %all-to-all-done = bf16[8,128,768]{2,1,0:T(8,128)(2,1)} async-done(((bf16[8,128,768]{2,1,0:T(8,128)(2,1)}), bf16[8,128,768]{2,1,0:T(8,128)(2,1)}, u32[]{:S(2)}, u32[]{:S(2)}) %all-to-all-start) | async-done | bytes 1572896 | tf_op jit(solution)/shard_map/all_to_all | solution.py:119
  126.2 4.3 all-to-all-start.2
  130.6 10.3 %fusion.19 = f32[1024,3072]{1,0:T(8,128)} fusion(bf16[1024,768]{1,0:T(8,128)(2,1)} %bitcast.14, bf16[1,3072,768]{2,1,0:T(8,128)(2,1)} %all-gather.3.cloned.1.call-done), kind=kOutput, calls=%fused_computation.32 | convolution fusion | flops 4831838208 | bytes 18874368 | tf_op jit(solution)/shard_map/gcd,gfd->gcf/dot_general | solution.py:19
  140.9 26.3 %all-to-all-done.2 = bf16[8,128,768]{2,1,0:T(8,128)(2,1)} async-done(((bf16[8,128,768]{2,1,0:T(8,128)(2,1)}), bf16[8,128,768]{2,1,0:T(8,128)(2,1)}, u32[]{:S(2)}, u32[]{:S(2)}) %all-to-all-start.2) | async-done | bytes 1572896 | tf_op jit(solution)/shard_map/all_to_all | solution.py:138
  167.2 11.3 %fusion.98 = f32[3072,768]{0,1:T(8,128)} fusion(bf16[1024,768]{1,0:T(8,128)(2,1)} %bitcast.22, f32[1024,3072]{1,0:T(8,128)} %fusion.19), kind=kOutput, calls=%fused_computation.147 | convolution fusion | flops 4860149760 | bytes 23592960 | tf_op jit(solution)/shard_map/dot_general | solution.py:164
  178.5 15.7 %fusion.6 = bf16[1024,3072]{1,0:T(8,128)(2,1)S(1)} fusion(f32[1024,3072]{1,0:T(8,128)} %fusion.19, bf16[1024,768]{1,0:T(8,128)(2,1)} %bitcast.22, bf16[1,3072,768]{2,1,0:T(8,128)(2,1)} %all-gather.5.cloned.1.call-done), kind=kOutput, calls=%fused_computation.13 | convolution fusion | flops 4894752768 | bytes 25165824 | tf_op jit(solution)/shard_map/gcd,gfd->gcf/dot_general | solution.py:28
  194.3 8.3 %fusion.105 = f32[3072,768]{0,1:T(8,128)S(1)} fusion(bf16[1024,3072]{1,0:T(8,128)(2,1)S(1)} %fusion.6, bf16[1024,768]{1,0:T(8,128)(2,1)} %bitcast.14), kind=kOutput, calls=%fused_computation.153 | convolution fusion | flops 4831838208 | bytes 17301504 | tf_op jit(solution)/shard_map/dot_general | solution.py:161
  202.6 6.9 %pad_maximum_fusion = f32[3072,1536]{0,1:T(8,128)} fusion(f32[3072,768]{0,1:T(8,128)S(1)} %copy-done.11, f32[3072,768]{0,1:T(8,128)S(1)} %fusion.105), kind=kLoop, calls=%fused_computation.4 | loop fusion | flops 4718592 | bytes 37748736 | tf_op jit(solution)/shard_map/concatenate | solution.py:168
  209.5 12.5 %fusion.40 = bf16[1024,768]{1,0:T(8,128)(2,1)} fusion(bf16[1,3072,768]{2,1,0:T(8,128)(2,1)} %all-gather.5.cloned.1.call-done, f32[1024,3072]{1,0:T(8,128)} %fusion.19), kind=kOutput, calls=%fused_computation.65 | convolution fusion | flops 4860936192 | bytes 18874368 | tf_op jit(solution)/shard_map/gcf,gfd->gcd/dot_general | solution.py:21
  222.0 4.5 all-to-all-start.1
  229.5 8.9 %fusion.104 = f32[2,128,3072]{2,1,0:T(8,128)S(1)} fusion(bf16[2,128,768]{2,1,0:T(8,128)(2,1)S(1)} %bitcast.104, bf16[2,3072,768]{2,1,0:T(8,128)(2,1)} %param.24), kind=kOutput, calls=%fused_computation.152 | convolution fusion | flops 1207959552 | bytes 12976128 | tf_op jit(solution)/shard_map/gcd,gfd->gcf/dot_general | solution.py:19
  238.4 7.5 %fusion.63 = bf16[2,128,768]{2,1,0:T(8,128)(2,1)} fusion(bf16[2,3072,768]{2,1,0:T(8,128)(2,1)} %param.25, f32[2,128,3072]{2,1,0:T(8,128)S(1)} %fusion.104), kind=kOutput, calls=%fused_computation.91 | convolution fusion | flops 1215234048 | bytes 12976128 | tf_op jit(solution)/shard_map/gcf,gfd->gcd/dot_general | solution.py:21
  246.0 6.1 %fusion.37 = bf16[1024,768]{1,0:T(8,128)(2,1)} fusion(bf16[1024,3072]{1,0:T(8,128)(2,1)S(1)} %bitcast.128, bf16[1,3072,768]{2,1,0:T(8,128)(2,1)S(1)} %bitcast.123), kind=kOutput, calls=%fused_computation.64 | convolution fusion | flops 4832624640 | bytes 12582912 | tf_op jit(solution)/shard_map/gcf,gfd->gcd/dot_general | solution.py:33
  252.1 11.0 %all-to-all-done.1 = bf16[8,128,768]{2,1,0:T(8,128)(2,1)} async-done(((bf16[8,128,768]{2,1,0:T(8,128)(2,1)}), bf16[8,128,768]{2,1,0:T(8,128)(2,1)}, u32[]{:S(2)}, u32[]{:S(2)}) %all-to-all-start.1) | async-done | bytes 1572896 | tf_op jit(solution)/shard_map/all_to_all | solution.py:125
  263.1 4.3 all-to-all-start.3
  268.9 13.3 %fusion.60 = bf16[2,128,768]{2,1,0:T(8,128)(2,1)} fusion(bf16[2,3072,768]{2,1,0:T(8,128)(2,1)} %param.24, f32[2,128,3072]{2,1,0:T(8,128)} %copy-done.19, bf16[2,128,768]{2,1,0:T(8,128)(2,1)} %bitcast.111, bf16[2,3072,768]{2,1,0:T(8,128)(2,1)} %param.25), kind=kOutput, calls=%fused_computation.90 | convolution fusion | flops 2431844352 | bytes 22806528 | tf_op jit(solution)/shard_map/gcf,gfd->gcd/dot_general | solution.py:33
  285.1 7.6 %gather_fusion = bf16[1024,768]{1,0:T(8,128)(2,1)} fusion(bf16[1280,768]{1,0:T(8,128)(2,1)} %pad_maximum_fusion.2, s32[1024]{0:T(1024)S(1)} %broadcast_clamp_fusion), kind=kCustom, calls=%fused_computation | custom fusion | bytes 3149824 | tf_op jit(solution)/shard_map/gather | solution.py:129
  292.7 11.4 %all-to-all-done.3 = bf16[8,128,768]{2,1,0:T(8,128)(2,1)} async-done(((bf16[8,128,768]{2,1,0:T(8,128)(2,1)}), bf16[8,128,768]{2,1,0:T(8,128)(2,1)}, u32[]{:S(2)}, u32[]{:S(2)}) %all-to-all-start.3) | async-done | bytes 1572896 | tf_op jit(solution)/shard_map/all_to_all | solution.py:147
  307.0 7.4 %gather_fusion.1 = bf16[1024,768]{1,0:T(8,128)(2,1)} fusion(bf16[1280,768]{1,0:T(8,128)(2,1)} %pad_maximum_fusion.3, s32[1024]{0:T(1024)S(1)} %broadcast_clamp_fusion), kind=kCustom, calls=%fused_computation.1 | custom fusion | bytes 3149824 | tf_op jit(solution)/shard_map/gather | solution.py:176
  314.4 4.9 reshape.386
  319.3 4.9 reshape.385
  324.2 6.8 %reduce_sum.185 = f32[512,768]{1,0:T(8,128)} reduce(f32[512,2,768]{2,1,0:T(2,128)} %reshape.386, f32[]{:T(128)} %constant.18.clone.1), dimensions={1}, to_apply=%region_14.15 | reduce | flops 393216 | bytes 4718596 | tf_op jit(solution)/shard_map/reduce_sum | solution.py:175
  330.9 3.2 multiply_reduce_fusion.2
  334.2 16.6 %multiply_reduce_fusion.1 = f32[512,768]{1,0:T(8,128)S(1)} fusion(f32[512,2,768]{2,1,0:T(2,128)S(1)} %copy-done.6, f32[512,2]{1,0:T(8,128)} %copy.66), kind=kLoop, calls=%fused_computation.46 | loop fusion | flops 1179648 | bytes 4722688 | tf_op jit(solution)/shard_map/reduce_sum | solution.py:130
  357.6 4.3 fusion.72
  362.0 11.0 %multiply_reduce_fusion = (f32[12,512]{1,0:T(8,128)S(1)}, f32[12,512,512]{1,2,0:T(8,128)}) fusion(f32[12,512]{1,0:T(8,128)S(1)} %copy-done.25, f32[12,512,512]{1,2,0:T(8,128)} %copy-done.1, pred[512,512]{0,1:T(8,128)(4,1)S(1)} %copy-done.15, bf16[512,12,64]{0,2,1:T(8,128)(2,1)S(1)} %bitcast.100, bf16[512,12,64]{0,2,1:T(8,128)(2,1)S(1)} %bitcast.99), kind=kOutput, calls=%fused_computation.15 | convolution fusion | flops 418375680 | bytes 27049984 | tf_op jit(solution)/shard_map/qhd,khd->hqk/dot_general | solution.py:195
  374.5 7.0 %multiply_convert_fusion = bf16[12,512,512]{1,2,0:T(8,128)(2,1)S(1)} fusion(f32[12,512,512]{1,2,0:T(8,128)} %get-tuple-element.60, f32[12,512]{1,0:T(8,128)S(1)} %get-tuple-element.59, f32[12,512]{1,0:T(8,128)S(1)} %copy-done.25, f32[12,512,512]{1,2,0:T(8,128)S(1)} %bitcast.91, pred[512,512]{0,1:T(8,128)(4,1)S(1)} %copy-done.15), kind=kLoop, calls=%fused_computation.14 | loop fusion | flops 18874368 | bytes 31768576 | tf_op jit(solution)/shard_map/convert_element_type | solution.py:199
  385.7 3.3 fusion.56
  389.9 5.3 fusion.70
  396.5 4.2 fusion.46
  402.1 40.2 %all-reduce = (f32[768]{0:T(1024)}, f32[768]{0:T(1024)}, f32[10]{0:T(128)}) all-reduce(f32[768]{0:T(1024)} %get-tuple-element.38, f32[768]{0:T(1024)} %get-tuple-element.36, f32[10]{0:T(128)} %convert_element_type.136), channel_id=1, replica_groups=mesh['dp'=4,'expert'=8] {'dp','expert'}, use_global_device_ids=true, to_apply=%region_21.22 | all-reduce | flops 1546 | bytes 12368 | tf_op jit(solution)/shard_map/psum | solution.py:228
  442.9 4.0 add_convert_fusion
  446.9 5.0 slice_bitcast_fusion
  451.9 3.0 copy.73
  458.0 128.8 %all-reduce.4.cloned.1.call-done = (f32[768,2304]{1,0:T(8,128)}, f32[768,768]{1,0:T(8,128)}) async-done(((f32[768,2304]{1,0:T(8,128)}, f32[768,768]{1,0:T(8,128)}), (f32[768,2304]{1,0:T(8,128)}, f32[768,768]{1,0:T(8,128)})) %all-reduce.4.cloned.1.call-update) | async-done | bytes 9437200 | tf_op jit(solution)/shard_map/psum | solution.py:228
  586.8 6.6 %copy.81 = f32[768,2304]{1,0:T(8,128)} copy(f32[768,2304]{1,0:T(8,128)} %get-tuple-element.66) | data formatting | bytes 14155776
  (186 shorter events, 72.8 us)
Async XLA Ops:
  7.2 20.0 %copy-start = (bf16[768,2304]{1,0:T(8,128)(2,1)S(1)}, bf16[768,2304]{1,0:T(8,128)(2,1)}, u32[]{:S(2)}) copy-start(bf16[768,2304]{1,0:T(8,128)(2,1)} %param.21) | copy-start | bytes 10616836
  7.2 123.4 %all-gather.3.cloned.1.call-start = ((), (), s32[]{:S(2)}) async-start(), calls=%async_computation.5 | async-start | bytes 5898240 | tf_op jit(solution)/shard_map/all_gather | solution.py:70
  9.6 22.3 %copy-start.31 = (f32[512]{0:T(512)}, f32[512]{0:T(512)S(1)}, u32[]{:S(2)}) copy-start(f32[512]{0:T(512)S(1)} %broadcast_multiply_fusion.2) | copy-start | bytes 6148
  11.1 12.5 %copy-start.37 = (f32[512]{0:T(512)}, f32[512]{0:T(512)S(1)}, u32[]{:S(2)}) copy-start(f32[512]{0:T(512)S(1)} %fusion.45) | copy-start | bytes 6148
  11.1 20.7 %copy-start.35 = (f32[512]{0:T(512)}, f32[512]{0:T(512)S(1)}, u32[]{:S(2)}) copy-start(f32[512]{0:T(512)S(1)} %fusion.77) | copy-start | bytes 6148
  27.1 4.7 copy-start.41
  40.3 7.0 %copy-start.45 = (s32[512]{0:T(512)S(1)}, s32[512]{0:T(512)}, u32[]{:S(2)}) copy-start(s32[512]{0:T(512)} %param.19) | copy-start | bytes 6148
  51.1 4.6 copy-start.1
  51.1 4.6 copy-start.24
  54.9 5.9 copy-start.26
  55.7 5.1 copy-start.7
  55.7 5.1 copy-start.46
  79.1 10.7 %copy-start.44 = (f32[512,2]{0,1:T(2,128)S(1)}, f32[512,2]{0,1:T(2,128)}, u32[]{:S(2)}) copy-start(f32[512,2]{0,1:T(2,128)} %param.17) | copy-start | bytes 12292
  81.8 44.5 %all-to-all-start = ((bf16[8,128,768]{2,1,0:T(8,128)(2,1)}), bf16[8,128,768]{2,1,0:T(8,128)(2,1)}, u32[]{:S(2)}, u32[]{:S(2)}) async-start(bf16[8,128,768]{2,1,0:T(8,128)(2,1)} %bitcast.96), calls=%async_computation | async-start | bytes 3145728 | tf_op jit(solution)/shard_map/all_to_all | solution.py:119
  89.1 89.4 %all-gather.5.cloned.1.call-start = ((), (), s32[]{:S(2)}) async-start(), calls=%async_computation.6 | async-start | bytes 5898240 | tf_op jit(solution)/shard_map/all_gather | solution.py:71
  126.2 40.9 %all-to-all-start.2 = ((bf16[8,128,768]{2,1,0:T(8,128)(2,1)}), bf16[8,128,768]{2,1,0:T(8,128)(2,1)}, u32[]{:S(2)}, u32[]{:S(2)}) async-start(bf16[8,128,768]{2,1,0:T(8,128)(2,1)} %bitcast.97), calls=%async_computation.2 | async-start | bytes 3145728 | tf_op jit(solution)/shard_map/all_to_all | solution.py:138
  130.5 316.4 %reduce-scatter.2.cloned.1.call-start = ((), (), s32[]{:S(2)}) async-start(), calls=%async_computation.7 | async-start | bytes 23592960 | tf_op jit(solution)/shard_map/reduce_scatter | solution.py:167
  194.3 8.3 %copy-start.49 = (bf16[1024,3072]{1,0:T(8,128)(2,1)}, bf16[1024,3072]{1,0:T(8,128)(2,1)S(1)}, u32[]{:S(2)}) copy-start(bf16[1024,3072]{1,0:T(8,128)(2,1)S(1)} %fusion.6) | copy-start | bytes 18874372
  194.3 8.3 %copy-start.11 = (f32[3072,768]{0,1:T(8,128)S(1)}, f32[3072,768]{0,1:T(8,128)}, u32[]{:S(2)}) copy-start(f32[3072,768]{0,1:T(8,128)} %fusion.98) | copy-start | bytes 28311556
  222.0 41.1 %all-to-all-start.1 = ((bf16[8,128,768]{2,1,0:T(8,128)(2,1)}), bf16[8,128,768]{2,1,0:T(8,128)(2,1)}, u32[]{:S(2)}, u32[]{:S(2)}) async-start(bf16[8,128,768]{2,1,0:T(8,128)(2,1)} %bitcast.106), calls=%async_computation.1 | async-start | bytes 3145728 | tf_op jit(solution)/shard_map/all_to_all | solution.py:125
  229.5 16.4 %slice-start.3 = ((s8[4718592]{0:T(1024)(128)(4,1)}), s8[524288]{0:T(1024)(128)(4,1)S(1)}, s32[]{:S(2)}) async-start(s8[4718592]{0:T(1024)(128)(4,1)} %bitcast.122), calls=%async_computation.12 | async-start | bytes 1048576
  229.5 16.4 %slice-start.5 = ((s8[6291456]{0:T(1024)(128)(4,1)}), s8[4194304]{0:T(1024)(128)(4,1)S(1)}, s32[]{:S(2)}) async-start(s8[6291456]{0:T(1024)(128)(4,1)} %bitcast.127), calls=%async_computation.14 | async-start | bytes 8388608
  238.4 7.5 %copy-start.19 = (f32[2,128,3072]{2,1,0:T(8,128)}, f32[2,128,3072]{2,1,0:T(8,128)S(1)}, u32[]{:S(2)}) copy-start(f32[2,128,3072]{2,1,0:T(8,128)S(1)} %fusion.104) | copy-start | bytes 9437188
  238.4 7.5 %slice-start.4 = ((s8[4718592]{0:T(1024)(128)(4,1)}), s8[4194304]{0:T(1024)(128)(4,1)S(1)}, s32[]{:S(2)}) async-start(s8[4718592]{0:T(1024)(128)(4,1)} %bitcast.122), calls=%async_computation.13 | async-start | bytes 8388608
  238.4 7.5 %slice-start.6 = ((s8[6291456]{0:T(1024)(128)(4,1)}), s8[2097152]{0:T(1024)(128)(4,1)S(1)}, s32[]{:S(2)}) async-start(s8[6291456]{0:T(1024)(128)(4,1)} %bitcast.127), calls=%async_computation.15 | async-start | bytes 4194304
  263.1 40.9 %all-to-all-start.3 = ((bf16[8,128,768]{2,1,0:T(8,128)(2,1)}), bf16[8,128,768]{2,1,0:T(8,128)(2,1)}, u32[]{:S(2)}, u32[]{:S(2)}) async-start(bf16[8,128,768]{2,1,0:T(8,128)(2,1)} %bitcast.105), calls=%async_computation.3 | async-start | bytes 3145728 | tf_op jit(solution)/shard_map/all_to_all | solution.py:147
  267.5 319.3 %all-reduce.4.cloned.1.call-start = ((), (), s32[]{:S(2)}) async-start(), calls=%async_computation.8 | async-start | bytes 18874368 | tf_op jit(solution)/shard_map/psum | solution.py:228
  324.1 6.8 %copy-start.28 = (f32[512]{0:T(512)S(1)}, f32[512]{0:T(512)}, u32[]{:S(2)}) copy-start(f32[512]{0:T(512)} %copy-done.27) | copy-start | bytes 6148
  324.1 6.8 %copy-start.30 = (f32[768]{0:T(1024)S(1)}, f32[768]{0:T(1024)}, u32[]{:S(2)}) copy-start(f32[768]{0:T(1024)} %param.23) | copy-start | bytes 9220
  324.1 6.8 %copy-start.34 = (f32[512]{0:T(512)S(1)}, f32[512]{0:T(512)}, u32[]{:S(2)}) copy-start(f32[512]{0:T(512)} %copy-done.33) | copy-start | bytes 6148
  324.1 10.0 %copy-start.40 = (f32[512]{0:T(512)S(1)}, f32[512]{0:T(512)}, u32[]{:S(2)}) copy-start(f32[512]{0:T(512)} %copy-done.39) | copy-start | bytes 6148
  334.1 16.7 %copy-start.3 = (f32[512,768]{1,0:T(8,128)S(1)}, f32[512,768]{1,0:T(8,128)}, u32[]{:S(2)}) copy-start(f32[512,768]{1,0:T(8,128)} %copy-done.2) | copy-start | bytes 4718596
  334.2 16.7 %copy-start.4 = (f32[512,768]{1,0:T(8,128)S(1)}, f32[512,768]{1,0:T(8,128)}, u32[]{:S(2)}) copy-start(f32[512,768]{1,0:T(8,128)} %reduce_sum.185) | copy-start | bytes 4718596
  357.6 4.3 copy-start.15
  357.6 4.3 copy-start.17
  357.6 4.3 copy-start.18
  357.6 4.3 copy-start.25
  361.9 11.1 %slice-start = ((s8[12582912]{0:T(1024)(128)(4,1)}), s8[4194304]{0:T(1024)(128)(4,1)S(1)}, s32[]{:S(2)}) async-start(s8[12582912]{0:T(1024)(128)(4,1)} %bitcast.90), calls=%async_computation.9 | async-start | bytes 8388608
  361.9 11.1 %slice-start.1 = ((s8[12582912]{0:T(1024)(128)(4,1)}), s8[4194304]{0:T(1024)(128)(4,1)S(1)}, s32[]{:S(2)}) async-start(s8[12582912]{0:T(1024)(128)(4,1)} %bitcast.90), calls=%async_computation.10 | async-start | bytes 8388608
  361.9 12.6 %slice-start.2 = ((s8[12582912]{0:T(1024)(128)(4,1)}), s8[4194304]{0:T(1024)(128)(4,1)S(1)}, s32[]{:S(2)}) async-start(s8[12582912]{0:T(1024)(128)(4,1)} %bitcast.90), calls=%async_computation.11 | async-start | bytes 8388608
  374.5 7.1 %copy-start.12 = (bf16[512,768]{0,1:T(8,128)(2,1)S(1)}, bf16[512,768]{0,1:T(8,128)(2,1)}, u32[]{:S(2)}) copy-start(bf16[512,768]{0,1:T(8,128)(2,1)} %copy.58) | copy-start | bytes 2359300
  385.7 4.3 copy-start.8
  385.7 4.3 copy-start.23
  385.7 4.2 copy-start.32
  385.7 4.2 copy-start.36
  385.7 4.2 copy-start.42
  396.5 4.2 copy-start.43
  586.8 6.6 %copy-start.21 = (f32[768,768]{1,0:T(8,128)S(1)}, f32[768,768]{1,0:T(8,128)}, u32[]{:S(2)}) copy-start(f32[768,768]{1,0:T(8,128)} %get-tuple-element.67) | copy-start | bytes 7077892
  (17 other events, 38.1 us)
Sparse Core Ops, SparseCore 0:
  9.6 40.1 all-gather.2
  91.5 38.8 all-gather.4
  209.6 138.4 reduce-scatter.1
  395.4 191.3 all-reduce.3
where the time goes:
time: 612 us; the launch traced here: 601 us
  waiting for transfers between devices  194 us (32%)
  matrix products  142 us (23%)
  local copies, waits for them, and re-layouts  107 us (17%)
  other arithmetic  83.7 us (14%)
  blocking collectives  40.2 us (7%)
  starting transfers between devices  20.6 us (3%)
  between operations  14.7 us (2%)
    psum x1, waiting for transfers between devices, body(): lax.psum((gain1_grad, w_qkv_grad, w_o_grad, gain2_grad, local_counts), ('...  129 us
    psum x1, blocking collectives, body(): lax.psum((gain1_grad, w_qkv_grad, w_o_grad, gain2_grad, local_counts), ('...  40.2 us
    all_to_all x1, waiting for transfers between devices, body(): lax.all_to_all(routed_grad, 'expert', split_axis=0, concat_axis=0, tiled=...  26.3 us
    unnamed x122, local copies, waits for them, and re-layouts  23.9 us
    dot_general x2, matrix products, expert_forward(): jnp.einsum('gcf,gfd->gcd', active, down_weights, preferred_element_type=j...  20 us
    dot_general x2, matrix products, expert_backward(): jnp.einsum('gcf,gfd->gcd', hidden_grad, up_weights, preferred_element_typ...  19.5 us
    dot_general x2, matrix products, expert_forward(): jnp.einsum('gcd,gfd->gcf', rows_low, up_weights, preferred_element_type=j...  19.2 us
    reduce_sum x1, other arithmetic, body(): output = mixed_rows + jnp.sum(picked * gates[:, :, None], axis=1)  16.6 us
  transfers between devices with their start and end apart: 8, of which 5 were waited for; matrix products, arithmetic and copies ran while one was open for 48% of the time, Pallas kernels for 0%

commit v1 on v0

--- a/solution.py
+++ b/solution.py
@@ -1,3 +1,4 @@
+import functools
 import jax
 import jax.numpy as jnp
 from jax import lax
@@ -6,6 +7,32 @@
 HEADS = 12
 HEAD_DIM = 64
 FROZEN = 2
+
+
+def meet_waves(m, peer_axis):
+    passed = jax.lax.axis_size(peer_axis)
+    t1 = jax.lax.axis_index(peer_axis)
+    finding, everything = (passed, t1)
+    parts_out = m.shape[0] // finding
+    reached = list(m.shape)
+    reached[0] = parts_out
+    view_out = reached[0]
+    reached[0] = view_out * finding
+    arr_next = jnp.zeros(reached, m.dtype)
+    for rr in range(finding):
+        w1 = lax.dynamic_slice_in_dim(m, (everything ^ rr) * parts_out, parts_out, axis=0)
+        if rr:
+            wide_out = range(finding)
+            raw_out = map(lambda h: (h, h ^ rr), wide_out)
+            last = list(raw_out)
+            w1 = jax.lax.ppermute(w1, peer_axis, last)
+        arr_next = lax.dynamic_update_slice_in_dim(
+            arr_next, w1, (everything ^ rr) * view_out, axis=0
+        )
+    return arr_next
+
+
+begin_stops_all_by_axis = functools.partial(meet_waves, peer_axis="expert")
 
 
 def layer_norm(values_in, gain_vec):
@@ -135,7 +162,7 @@
     )
     frozen_grad_rows = grad_buffer[: FROZEN * slot_count].reshape(FROZEN, slot_count, feat_width)
     routed_grad = grad_buffer[FROZEN * slot_count :].reshape(owners, slot_count, feat_width)
-    arrived_grad = lax.all_to_all(routed_grad, "expert", split_axis=0, concat_axis=0, tiled=True)
+    arrived_grad = begin_stops_all_by_axis(routed_grad)
     flat_rows = arrived_rows.reshape(1, -1, feat_width)
     flat_grad = arrived_grad.reshape(1, -1, feat_width)
     hidden_all = jnp.einsum(

time: 612 us -> 620 us (1.013)
  local copies, waits for them, and re-layouts: 107 us -> 119 us
  waiting for transfers between devices: 194 us -> 187 us
    ppermute x0 -> x7, waiting for transfers between devices: none -> 34.4 us  [meet_waves(): w1 = jax.lax.ppermute(w1, peer_axis, last)]
    all_to_all x1 -> x0, waiting for transfers between devices: 26.3 us -> none  [body(): lax.all_to_all(routed_grad, 'expert', split_axis=0, concat_axis=0, tiled=...]
    all_to_all x1, waiting for transfers between devices: 14.8 us -> 0.01 us  [body(): lax.all_to_all(routed_rows, 'expert', split_axis=0, concat_axis=0, tiled=...]
    ppermute x0 -> x7, starting transfers between devices: none -> 9.43 us  [meet_waves(): w1 = jax.lax.ppermute(w1, peer_axis, last)]
    unnamed x122 -> x124, local copies, waits for them, and re-layouts: 23.9 us -> 28.8 us
  transfers between devices with their start and end apart: 8 -> 14, of which waited for: 5 -> 7; matrix products, arithmetic and copies ran while one was open for 48% -> 48% of each run, Pallas kernels for 0% -> 0%
where the time goes in v1:
time: 620 us; the launch traced here: 610 us
  waiting for transfers between devices  187 us (30%)
  matrix products  136 us (22%)
  local copies, waits for them, and re-layouts  119 us (19%)
  other arithmetic  87.7 us (14%)
  blocking collectives  40.2 us (6%)
  starting transfers between devices  25.6 us (4%)
  between operations  14.7 us (2%)
    psum x1, waiting for transfers between devices, body(): lax.psum((gain1_grad, w_qkv_grad, w_o_grad, gain2_grad, local_counts), ('...  129 us
    psum x1, blocking collectives, body(): lax.psum((gain1_grad, w_qkv_grad, w_o_grad, gain2_grad, local_counts), ('...  40.2 us
    ppermute x7, waiting for transfers between devices, meet_waves(): w1 = jax.lax.ppermute(w1, peer_axis, last)  34.4 us
    unnamed x124, local copies, waits for them, and re-layouts  28.8 us
    dot_general x2, matrix products, expert_forward(): jnp.einsum('gcf,gfd->gcd', active, down_weights, preferred_element_type=j...  20 us
    dot_general x2, matrix products, expert_backward(): jnp.einsum('gcf,gfd->gcd', hidden_grad, up_weights, preferred_element_typ...  19.5 us
    reduce_sum x1, other arithmetic, body(): output = mixed_rows + jnp.sum(picked * gates[:, :, None], axis=1)  16.6 us
    dot_general x2, matrix products, expert_forward(): jnp.einsum('gcd,gfd->gcf', rows_low, up_weights, preferred_element_type=j...  16.5 us
  transfers between devices with their start and end apart: 14, of which 7 were waited for; matrix products, arithmetic and copies ran while one was open for 48% of the time, Pallas kernels for 0%

profile of v1, /device:TPU:0, one launch (start us, length us, event | category | flops | bytes accessed | tf_op | source)
XLA Modules:
  0.0 610.3 jit_solution(12483238784258250351)
XLA Ops:
  18.8 6.2 %reduce-window.19 = s32[10,8,128]{2,1,0:T(8,128)} reduce-window(s32[10,8,128]{2,1,0:T(8,128)} %fusion.76, s32[]{:T(128)} %constant.30.clone.1), window={size=1x1x128 pad=0_0x0_0x127_0}, to_apply=%region_6.7 | reduce-window | flops 1300480 | bytes 81924 | tf_op jit(solution)/shard_map/reduce-window.1
  31.6 3.3 convolution_convert_fusion
  43.5 3.5 fusion.21
  47.1 3.7 fusion.7
  51.7 5.1 fusion.59
  68.6 4.6 reshape.407
  74.8 7.3 %scatter_custom_fusion = bf16[1280,768]{1,0:T(8,128)(2,1)} fusion(s32[1024]{0:T(1024)S(1)} %bitcast.116, bf16[1024,768]{1,0:T(8,128)(2,1)} %reshape.407, bf16[]{:T(256)} %constant.34.clone.1), kind=kCustom, calls=%fused_computation.98 | custom fusion | bytes 1966592 | tf_op jit(solution)/shard_map/scatter | solution.py:142
  84.7 7.3 %all-to-all-start = ((bf16[8,128,768]{2,1,0:T(8,128)(2,1)}), bf16[8,128,768]{2,1,0:T(8,128)(2,1)}, u32[]{:S(2)}, u32[]{:S(2)}) async-start(bf16[8,128,768]{2,1,0:T(8,128)(2,1)} %bitcast.96), calls=%async_computation | async-start | bytes 3145728 | tf_op jit(solution)/shard_map/all_to_all | solution.py:146
  94.0 3.6 broadcast_in_dim.37
  97.6 5.5 reshape.374
  103.1 7.8 %scatter_custom_fusion.1 = bf16[1280,768]{1,0:T(8,128)(2,1)} fusion(s32[1024]{0:T(1024)S(1)} %bitcast.117, f32[1024,768]{1,0:T(8,128)} %reshape.374, f32[1024]{0:T(1024)S(1)} %mul.298, bf16[]{:T(256)} %constant.34.clone.1), kind=kCustom, calls=%fused_computation.71 | custom fusion | flops 1572864 | bytes 5115906 | tf_op jit(solution)/shard_map/scatter | solution.py:161
  128.9 11.9 %collective-permute-done.1 = bf16[1,128,768]{2,1,0:T(8,128)(2,1)S(1)} collective-permute-done((bf16[1,128,768]{2,1,0:T(8,128)(2,1)S(1)}, bf16[1,128,768]{2,1,0:T(8,128)(2,1)S(1)}, u32[]{:S(2)}, u32[]{:S(2)}) %collective-permute-start.1) | collective-permute-done | bytes 196640 | tf_op jit(solution)/shard_map/ppermute | solution.py:28
  143.0 20.1 %collective-permute-done.3 = bf16[1,128,768]{2,1,0:T(8,128)(2,1)S(1)} collective-permute-done((bf16[1,128,768]{2,1,0:T(8,128)(2,1)S(1)}, bf16[1,128,768]{2,1,0:T(8,128)(2,1)S(1)}, u32[]{:S(2)}, u32[]{:S(2)}) %collective-permute-start.3) | collective-permute-done | bytes 196640 | tf_op jit(solution)/shard_map/ppermute | solution.py:28
  165.8 7.7 %fusion.19 = f32[1024,3072]{1,0:T(8,128)S(1)} fusion(bf16[1024,768]{1,0:T(8,128)(2,1)} %bitcast.14, bf16[1,3072,768]{2,1,0:T(8,128)(2,1)} %all-gather.3.cloned.1.call-done), kind=kOutput, calls=%fused_computation.32 | convolution fusion | flops 4831838208 | bytes 18874368 | tf_op jit(solution)/shard_map/gcd,gfd->gcf/dot_general | solution.py:46
  173.5 4.6 copy-done.49
  178.1 9.4 %fusion.98 = f32[3072,768]{0,1:T(8,128)} fusion(bf16[1024,768]{1,0:T(8,128)(2,1)} %bitcast.22, f32[1024,3072]{1,0:T(8,128)S(1)} %fusion.19), kind=kOutput, calls=%fused_computation.162 | convolution fusion | flops 4860149760 | bytes 23592960 | tf_op jit(solution)/shard_map/dot_general | solution.py:191
  187.5 15.8 %fusion.6 = bf16[1024,3072]{1,0:T(8,128)(2,1)S(1)} fusion(f32[1024,3072]{1,0:T(8,128)} %copy-done.49, bf16[1024,768]{1,0:T(8,128)(2,1)} %bitcast.22, bf16[1,3072,768]{2,1,0:T(8,128)(2,1)} %all-gather.5.cloned.1.call-done), kind=kOutput, calls=%fused_computation.13 | convolution fusion | flops 4894752768 | bytes 25165824 | tf_op jit(solution)/shard_map/gcd,gfd->gcf/dot_general | solution.py:55
  203.3 8.2 %fusion.105 = f32[3072,768]{0,1:T(8,128)S(1)} fusion(bf16[1024,3072]{1,0:T(8,128)(2,1)S(1)} %fusion.6, bf16[1024,768]{1,0:T(8,128)(2,1)} %bitcast.14), kind=kOutput, calls=%fused_computation.168 | convolution fusion | flops 4831838208 | bytes 17301504 | tf_op jit(solution)/shard_map/dot_general | solution.py:188
  211.6 7.0 %pad_maximum_fusion = f32[3072,1536]{0,1:T(8,128)} fusion(f32[3072,768]{0,1:T(8,128)S(1)} %copy-done.11, f32[3072,768]{0,1:T(8,128)S(1)} %fusion.105), kind=kLoop, calls=%fused_computation.4 | loop fusion | flops 4718592 | bytes 37748736 | tf_op jit(solution)/shard_map/concatenate | solution.py:195
  218.6 12.5 %fusion.40 = bf16[1024,768]{1,0:T(8,128)(2,1)} fusion(bf16[1,3072,768]{2,1,0:T(8,128)(2,1)} %all-gather.5.cloned.1.call-done, f32[1024,3072]{1,0:T(8,128)} %copy-done.49), kind=kOutput, calls=%fused_computation.65 | convolution fusion | flops 4860936192 | bytes 18874368 | tf_op jit(solution)/shard_map/gcf,gfd->gcd/dot_general | solution.py:48
  231.1 4.5 all-to-all-start.1
  238.5 8.8 %fusion.104 = f32[2,128,3072]{2,1,0:T(8,128)S(1)} fusion(bf16[2,128,768]{2,1,0:T(8,128)(2,1)S(1)} %bitcast.104, bf16[2,3072,768]{2,1,0:T(8,128)(2,1)} %param.24), kind=kOutput, calls=%fused_computation.167 | convolution fusion | flops 1207959552 | bytes 12976128 | tf_op jit(solution)/shard_map/gcd,gfd->gcf/dot_general | solution.py:46
  247.4 7.5 %fusion.63 = bf16[2,128,768]{2,1,0:T(8,128)(2,1)} fusion(bf16[2,3072,768]{2,1,0:T(8,128)(2,1)} %param.25, f32[2,128,3072]{2,1,0:T(8,128)S(1)} %fusion.104), kind=kOutput, calls=%fused_computation.91 | convolution fusion | flops 1215234048 | bytes 12976128 | tf_op jit(solution)/shard_map/gcf,gfd->gcd/dot_general | solution.py:48
  254.9 6.1 %fusion.37 = bf16[1024,768]{1,0:T(8,128)(2,1)} fusion(bf16[1024,3072]{1,0:T(8,128)(2,1)S(1)} %bitcast.128, bf16[1,3072,768]{2,1,0:T(8,128)(2,1)S(1)} %bitcast.123), kind=kOutput, calls=%fused_computation.64 | convolution fusion | flops 4832624640 | bytes 12582912 | tf_op jit(solution)/shard_map/gcf,gfd->gcd/dot_general | solution.py:60
  261.0 10.9 %all-to-all-done.1 = bf16[8,128,768]{2,1,0:T(8,128)(2,1)} async-done(((bf16[8,128,768]{2,1,0:T(8,128)(2,1)}), bf16[8,128,768]{2,1,0:T(8,128)(2,1)}, u32[]{:S(2)}, u32[]{:S(2)}) %all-to-all-start.1) | async-done | bytes 1572896 | tf_op jit(solution)/shard_map/all_to_all | solution.py:152
  272.0 4.3 all-to-all-start.2
  277.7 13.3 %fusion.60 = bf16[2,128,768]{2,1,0:T(8,128)(2,1)} fusion(bf16[2,3072,768]{2,1,0:T(8,128)(2,1)} %param.24, f32[2,128,3072]{2,1,0:T(8,128)} %copy-done.19, bf16[2,128,768]{2,1,0:T(8,128)(2,1)} %bitcast.111, bf16[2,3072,768]{2,1,0:T(8,128)(2,1)} %param.25), kind=kOutput, calls=%fused_computation.90 | convolution fusion | flops 2431844352 | bytes 22806528 | tf_op jit(solution)/shard_map/gcf,gfd->gcd/dot_general | solution.py:60
  293.9 7.6 %gather_fusion = bf16[1024,768]{1,0:T(8,128)(2,1)} fusion(bf16[1280,768]{1,0:T(8,128)(2,1)} %pad_maximum_fusion.2, s32[1024]{0:T(1024)S(1)} %broadcast_clamp_fusion), kind=kCustom, calls=%fused_computation | custom fusion | bytes 3149824 | tf_op jit(solution)/shard_map/gather | solution.py:156
  301.6 11.3 %all-to-all-done.2 = bf16[8,128,768]{2,1,0:T(8,128)(2,1)} async-done(((bf16[8,128,768]{2,1,0:T(8,128)(2,1)}), bf16[8,128,768]{2,1,0:T(8,128)(2,1)}, u32[]{:S(2)}, u32[]{:S(2)}) %all-to-all-start.2) | async-done | bytes 1572896 | tf_op jit(solution)/shard_map/all_to_all | solution.py:174
  315.8 7.4 %gather_fusion.1 = bf16[1024,768]{1,0:T(8,128)(2,1)} fusion(bf16[1280,768]{1,0:T(8,128)(2,1)} %pad_maximum_fusion.3, s32[1024]{0:T(1024)S(1)} %broadcast_clamp_fusion), kind=kCustom, calls=%fused_computation.1 | custom fusion | bytes 3149824 | tf_op jit(solution)/shard_map/gather | solution.py:203
  323.2 4.9 reshape.386
  328.1 4.9 reshape.385
  333.0 6.8 %reduce_sum.185 = f32[512,768]{1,0:T(8,128)} reduce(f32[512,2,768]{2,1,0:T(2,128)} %reshape.386, f32[]{:T(128)} %constant.27.clone.1), dimensions={1}, to_apply=%region_14.15 | reduce | flops 393216 | bytes 4718596 | tf_op jit(solution)/shard_map/reduce_sum | solution.py:202
  339.8 3.2 multiply_reduce_fusion.2
  343.0 16.6 %multiply_reduce_fusion.1 = f32[512,768]{1,0:T(8,128)S(1)} fusion(f32[512,2,768]{2,1,0:T(2,128)S(1)} %copy-done.6, f32[512,2]{1,0:T(8,128)} %copy.66), kind=kLoop, calls=%fused_computation.46 | loop fusion | flops 1179648 | bytes 4722688 | tf_op jit(solution)/shard_map/reduce_sum | solution.py:157
  366.4 4.3 fusion.72
  370.8 11.0 %multiply_reduce_fusion = (f32[12,512]{1,0:T(8,128)S(1)}, f32[12,512,512]{1,2,0:T(8,128)}) fusion(f32[12,512]{1,0:T(8,128)S(1)} %copy-done.25, f32[12,512,512]{1,2,0:T(8,128)} %copy-done.1, pred[512,512]{0,1:T(8,128)(4,1)S(1)} %copy-done.15, bf16[512,12,64]{0,2,1:T(8,128)(2,1)S(1)} %bitcast.100, bf16[512,12,64]{0,2,1:T(8,128)(2,1)S(1)} %bitcast.99), kind=kOutput, calls=%fused_computation.15 | convolution fusion | flops 418375680 | bytes 27049984 | tf_op jit(solution)/shard_map/qhd,khd->hqk/dot_general | solution.py:222
  383.4 7.0 %multiply_convert_fusion = bf16[12,512,512]{1,2,0:T(8,128)(2,1)S(1)} fusion(f32[12,512,512]{1,2,0:T(8,128)} %get-tuple-element.68, f32[12,512]{1,0:T(8,128)S(1)} %get-tuple-element.67, f32[12,512]{1,0:T(8,128)S(1)} %copy-done.25, f32[12,512,512]{1,2,0:T(8,128)S(1)} %bitcast.91, pred[512,512]{0,1:T(8,128)(4,1)S(1)} %copy-done.15), kind=kLoop, calls=%fused_computation.14 | loop fusion | flops 18874368 | bytes 31768576 | tf_op jit(solution)/shard_map/convert_element_type | solution.py:226
  394.5 3.3 fusion.56
  398.8 5.3 fusion.70
  405.3 4.2 fusion.46
  410.9 40.2 %all-reduce = (f32[768]{0:T(1024)}, f32[768]{0:T(1024)}, f32[10]{0:T(128)}) all-reduce(f32[768]{0:T(1024)} %get-tuple-element.38, f32[768]{0:T(1024)} %get-tuple-element.36, f32[10]{0:T(128)} %convert_element_type.136), channel_id=1, replica_groups=mesh['dp'=4,'expert'=8] {'dp','expert'}, use_global_device_ids=true, to_apply=%region_21.22 | all-reduce | flops 1546 | bytes 12368 | tf_op jit(solution)/shard_map/psum | solution.py:255
  451.8 4.0 add_convert_fusion
  455.8 5.0 slice_bitcast_fusion
  460.7 3.0 copy.73
  463.8 3.0 copy.72
  466.8 128.8 %all-reduce.4.cloned.1.call-done = (f32[768,2304]{1,0:T(8,128)}, f32[768,768]{1,0:T(8,128)}) async-done(((f32[768,2304]{1,0:T(8,128)}, f32[768,768]{1,0:T(8,128)}), (f32[768,2304]{1,0:T(8,128)}, f32[768,768]{1,0:T(8,128)})) %all-reduce.4.cloned.1.call-update) | async-done | bytes 9437200 | tf_op jit(solution)/shard_map/psum | solution.py:255
  595.6 6.6 %copy.89 = f32[768,2304]{1,0:T(8,128)} copy(f32[768,2304]{1,0:T(8,128)} %get-tuple-element.74) | data formatting | bytes 14155776
  (209 shorter events, 96.6 us)
Async XLA Ops:
  7.2 24.4 %copy-start = (bf16[768,2304]{1,0:T(8,128)(2,1)S(1)}, bf16[768,2304]{1,0:T(8,128)(2,1)}, u32[]{:S(2)}) copy-start(bf16[768,2304]{1,0:T(8,128)(2,1)} %param.21) | copy-start | bytes 10616836
  7.2 158.6 %all-gather.3.cloned.1.call-start = ((), (), s32[]{:S(2)}) async-start(), calls=%async_computation.4 | async-start | bytes 5898240 | tf_op jit(solution)/shard_map/all_gather | solution.py:97
  7.9 179.5 %all-gather.5.cloned.1.call-start = ((), (), s32[]{:S(2)}) async-start(), calls=%async_computation.5 | async-start | bytes 5898240 | tf_op jit(solution)/shard_map/all_gather | solution.py:98
  14.9 19.9 %copy-start.31 = (f32[512]{0:T(512)}, f32[512]{0:T(512)S(1)}, u32[]{:S(2)}) copy-start(f32[512]{0:T(512)S(1)} %broadcast_multiply_fusion.2) | copy-start | bytes 6148
  16.4 11.6 %copy-start.36 = (f32[512]{0:T(512)}, f32[512]{0:T(512)S(1)}, u32[]{:S(2)}) copy-start(f32[512]{0:T(512)S(1)} %fusion.45) | copy-start | bytes 6148
  36.3 7.0 %copy-start.45 = (pred[512]{0:T(512)(128)(4,1)S(1)}, pred[512]{0:T(512)(128)(4,1)}, u32[]{:S(2)}) copy-start(pred[512]{0:T(512)(128)(4,1)} %broadcast_compare_fusion) | copy-start | bytes 1540
  47.1 4.6 copy-start.1
  47.1 4.6 copy-start.24
  50.8 5.9 copy-start.26
  51.7 5.1 copy-start.7
  51.7 5.1 copy-start.46
  56.8 4.8 copy-start.41
  56.8 8.2 %copy-start.29 = (f32[768]{0:T(1024)S(1)}, f32[768]{0:T(1024)}, u32[]{:S(2)}) copy-start(f32[768]{0:T(1024)} %param.23) | copy-start | bytes 9220
  57.7 10.9 %copy-start.27 = (f32[512]{0:T(512)}, f32[512]{0:T(512)S(1)}, u32[]{:S(2)}) copy-start(f32[512]{0:T(512)S(1)} %broadcast_multiply_fusion.1) | copy-start | bytes 6148
  59.8 13.5 %copy-start.33 = (f32[512]{0:T(512)}, f32[512]{0:T(512)S(1)}, u32[]{:S(2)}) copy-start(f32[512]{0:T(512)S(1)} %fusion.78) | copy-start | bytes 6148
  66.6 6.6 %copy-start.40 = (s32[1024]{0:T(1024)S(1)}, s32[1024]{0:T(1024)}, u32[]{:S(2)}) copy-start(s32[1024]{0:T(1024)} %eq.73) | copy-start | bytes 12292
  82.0 10.0 %copy-start.44 = (f32[512,2]{0,1:T(2,128)S(1)}, f32[512,2]{0,1:T(2,128)}, u32[]{:S(2)}) copy-start(f32[512,2]{0,1:T(2,128)} %param.17) | copy-start | bytes 12292
  84.7 81.1 %all-to-all-start = ((bf16[8,128,768]{2,1,0:T(8,128)(2,1)}), bf16[8,128,768]{2,1,0:T(8,128)(2,1)}, u32[]{:S(2)}, u32[]{:S(2)}) async-start(bf16[8,128,768]{2,1,0:T(8,128)(2,1)} %bitcast.96), calls=%async_computation | async-start | bytes 3145728 | tf_op jit(solution)/shard_map/all_to_all | solution.py:146
  92.0 363.8 %reduce-scatter.2.cloned.1.call-start = ((), (), s32[]{:S(2)}) async-start(), calls=%async_computation.6 | async-start | bytes 23592960 | tf_op jit(solution)/shard_map/reduce_scatter | solution.py:194
  117.1 10.3 %collective-permute-start = (bf16[1,128,768]{2,1,0:T(8,128)(2,1)S(1)}, bf16[1,128,768]{2,1,0:T(8,128)(2,1)S(1)}, u32[]{:S(2)}, u32[]{:S(2)}) collective-permute-start(bf16[1,128,768]{2,1,0:T(8,128)(2,1)S(1)} %get-tuple-element.61), channel_id=1, source_target_pairs={{0,1},{1,0},{2,3},{3,2},{4,5},{5,4},{6,7},{7,6},{8,9},{9,8},{10,11... | collective-permute-start | bytes 589832 | tf_op jit(solution)/shard_map/ppermute | solution.py:28
  119.1 21.7 %collective-permute-start.1 = (bf16[1,128,768]{2,1,0:T(8,128)(2,1)S(1)}, bf16[1,128,768]{2,1,0:T(8,128)(2,1)S(1)}, u32[]{:S(2)}, u32[]{:S(2)}) collective-permute-start(bf16[1,128,768]{2,1,0:T(8,128)(2,1)S(1)} %get-tuple-element.60), channel_id=1, source_target_pairs={{0,2},{1,3},{2,0},{3,1},{4,6},{5,7},{6,4},{7,5},{8,10},{9,11},{10,... | collective-permute-start | bytes 589832 | tf_op jit(solution)/shard_map/ppermute | solution.py:28
  120.5 44.6 %collective-permute-start.6 = (bf16[1,128,768]{2,1,0:T(8,128)(2,1)S(1)}, bf16[1,128,768]{2,1,0:T(8,128)(2,1)S(1)}, u32[]{:S(2)}, u32[]{:S(2)}) collective-permute-start(bf16[1,128,768]{2,1,0:T(8,128)(2,1)S(1)} %get-tuple-element.55), channel_id=1, source_target_pairs={{0,7},{1,6},{2,5},{3,4},{4,3},{5,2},{6,1},{7,0},{8,15},{9,14},{10,... | collective-permute-start | bytes 589832 | tf_op jit(solution)/shard_map/ppermute | solution.py:28
  122.9 41.5 %collective-permute-start.5 = (bf16[1,128,768]{2,1,0:T(8,128)(2,1)S(1)}, bf16[1,128,768]{2,1,0:T(8,128)(2,1)S(1)}, u32[]{:S(2)}, u32[]{:S(2)}) collective-permute-start(bf16[1,128,768]{2,1,0:T(8,128)(2,1)S(1)} %get-tuple-element.56), channel_id=1, source_target_pairs={{0,6},{1,7},{2,4},{3,5},{4,2},{5,3},{6,0},{7,1},{8,14},{9,15},{10,... | collective-permute-start | bytes 589832 | tf_op jit(solution)/shard_map/ppermute | solution.py:28
  124.4 39.4 %collective-permute-start.4 = (bf16[1,128,768]{2,1,0:T(8,128)(2,1)S(1)}, bf16[1,128,768]{2,1,0:T(8,128)(2,1)S(1)}, u32[]{:S(2)}, u32[]{:S(2)}) collective-permute-start(bf16[1,128,768]{2,1,0:T(8,128)(2,1)S(1)} %get-tuple-element.57), channel_id=1, source_target_pairs={{0,5},{1,4},{2,7},{3,6},{4,1},{5,0},{6,3},{7,2},{8,13},{9,12},{10,... | collective-permute-start | bytes 589832 | tf_op jit(solution)/shard_map/ppermute | solution.py:28
  127.4 14.8 %collective-permute-start.2 = (bf16[1,128,768]{2,1,0:T(8,128)(2,1)S(1)}, bf16[1,128,768]{2,1,0:T(8,128)(2,1)S(1)}, u32[]{:S(2)}, u32[]{:S(2)}) collective-permute-start(bf16[1,128,768]{2,1,0:T(8,128)(2,1)S(1)} %get-tuple-element.59), channel_id=1, source_target_pairs={{0,3},{1,2},{2,1},{3,0},{4,7},{5,6},{6,5},{7,4},{8,11},{9,10},{10,... | collective-permute-start | bytes 589832 | tf_op jit(solution)/shard_map/ppermute | solution.py:28
  140.8 22.3 %collective-permute-start.3 = (bf16[1,128,768]{2,1,0:T(8,128)(2,1)S(1)}, bf16[1,128,768]{2,1,0:T(8,128)(2,1)S(1)}, u32[]{:S(2)}, u32[]{:S(2)}) collective-permute-start(bf16[1,128,768]{2,1,0:T(8,128)(2,1)S(1)} %get-tuple-element.58), channel_id=1, source_target_pairs={{0,4},{1,5},{2,6},{3,7},{4,0},{5,1},{6,2},{7,3},{8,12},{9,13},{10,... | collective-permute-start | bytes 589832 | tf_op jit(solution)/shard_map/ppermute | solution.py:28
  173.5 4.6 copy-start.49
  203.3 8.3 %copy-start.50 = (bf16[1024,3072]{1,0:T(8,128)(2,1)}, bf16[1024,3072]{1,0:T(8,128)(2,1)S(1)}, u32[]{:S(2)}) copy-start(bf16[1024,3072]{1,0:T(8,128)(2,1)S(1)} %fusion.6) | copy-start | bytes 18874372
  203.3 8.3 %copy-start.11 = (f32[3072,768]{0,1:T(8,128)S(1)}, f32[3072,768]{0,1:T(8,128)}, u32[]{:S(2)}) copy-start(f32[3072,768]{0,1:T(8,128)} %fusion.98) | copy-start | bytes 28311556
  231.1 40.9 %all-to-all-start.1 = ((bf16[8,128,768]{2,1,0:T(8,128)(2,1)}), bf16[8,128,768]{2,1,0:T(8,128)(2,1)}, u32[]{:S(2)}, u32[]{:S(2)}) async-start(bf16[8,128,768]{2,1,0:T(8,128)(2,1)} %bitcast.106), calls=%async_computation.1 | async-start | bytes 3145728 | tf_op jit(solution)/shard_map/all_to_all | solution.py:152
  238.5 16.3 %slice-start.3 = ((s8[4718592]{0:T(1024)(128)(4,1)}), s8[524288]{0:T(1024)(128)(4,1)S(1)}, s32[]{:S(2)}) async-start(s8[4718592]{0:T(1024)(128)(4,1)} %bitcast.122), calls=%async_computation.11 | async-start | bytes 1048576
  238.5 16.3 %slice-start.5 = ((s8[6291456]{0:T(1024)(128)(4,1)}), s8[4194304]{0:T(1024)(128)(4,1)S(1)}, s32[]{:S(2)}) async-start(s8[6291456]{0:T(1024)(128)(4,1)} %bitcast.127), calls=%async_computation.13 | async-start | bytes 8388608
  247.3 7.5 %copy-start.19 = (f32[2,128,3072]{2,1,0:T(8,128)}, f32[2,128,3072]{2,1,0:T(8,128)S(1)}, u32[]{:S(2)}) copy-start(f32[2,128,3072]{2,1,0:T(8,128)S(1)} %fusion.104) | copy-start | bytes 9437188
  247.3 7.5 %slice-start.4 = ((s8[4718592]{0:T(1024)(128)(4,1)}), s8[4194304]{0:T(1024)(128)(4,1)S(1)}, s32[]{:S(2)}) async-start(s8[4718592]{0:T(1024)(128)(4,1)} %bitcast.122), calls=%async_computation.12 | async-start | bytes 8388608
  247.3 7.5 %slice-start.6 = ((s8[6291456]{0:T(1024)(128)(4,1)}), s8[2097152]{0:T(1024)(128)(4,1)S(1)}, s32[]{:S(2)}) async-start(s8[6291456]{0:T(1024)(128)(4,1)} %bitcast.127), calls=%async_computation.14 | async-start | bytes 4194304
  272.0 40.9 %all-to-all-start.2 = ((bf16[8,128,768]{2,1,0:T(8,128)(2,1)}), bf16[8,128,768]{2,1,0:T(8,128)(2,1)}, u32[]{:S(2)}, u32[]{:S(2)}) async-start(bf16[8,128,768]{2,1,0:T(8,128)(2,1)} %bitcast.105), calls=%async_computation.2 | async-start | bytes 3145728 | tf_op jit(solution)/shard_map/all_to_all | solution.py:174
  276.3 319.3 %all-reduce.4.cloned.1.call-start = ((), (), s32[]{:S(2)}) async-start(), calls=%async_computation.7 | async-start | bytes 18874368 | tf_op jit(solution)/shard_map/psum | solution.py:255
  333.0 6.8 %copy-start.28 = (f32[512]{0:T(512)S(1)}, f32[512]{0:T(512)}, u32[]{:S(2)}) copy-start(f32[512]{0:T(512)} %copy-done.27) | copy-start | bytes 6148
  333.0 6.8 %copy-start.30 = (f32[768]{0:T(1024)S(1)}, f32[768]{0:T(1024)}, u32[]{:S(2)}) copy-start(f32[768]{0:T(1024)} %param.23) | copy-start | bytes 9220
  333.0 6.8 %copy-start.34 = (f32[512]{0:T(512)S(1)}, f32[512]{0:T(512)}, u32[]{:S(2)}) copy-start(f32[512]{0:T(512)} %copy-done.33) | copy-start | bytes 6148
  333.0 10.0 %copy-start.39 = (f32[512]{0:T(512)S(1)}, f32[512]{0:T(512)}, u32[]{:S(2)}) copy-start(f32[512]{0:T(512)} %copy-done.38) | copy-start | bytes 6148
  343.0 16.7 %copy-start.3 = (f32[512,768]{1,0:T(8,128)S(1)}, f32[512,768]{1,0:T(8,128)}, u32[]{:S(2)}) copy-start(f32[512,768]{1,0:T(8,128)} %copy-done.2) | copy-start | bytes 4718596
  343.0 16.7 %copy-start.4 = (f32[512,768]{1,0:T(8,128)S(1)}, f32[512,768]{1,0:T(8,128)}, u32[]{:S(2)}) copy-start(f32[512,768]{1,0:T(8,128)} %reduce_sum.185) | copy-start | bytes 4718596
  370.7 11.1 %slice-start = ((s8[12582912]{0:T(1024)(128)(4,1)}), s8[4194304]{0:T(1024)(128)(4,1)S(1)}, s32[]{:S(2)}) async-start(s8[12582912]{0:T(1024)(128)(4,1)} %bitcast.90), calls=%async_computation.8 | async-start | bytes 8388608
  370.8 11.1 %slice-start.1 = ((s8[12582912]{0:T(1024)(128)(4,1)}), s8[4194304]{0:T(1024)(128)(4,1)S(1)}, s32[]{:S(2)}) async-start(s8[12582912]{0:T(1024)(128)(4,1)} %bitcast.90), calls=%async_computation.9 | async-start | bytes 8388608
  370.8 12.6 %slice-start.2 = ((s8[12582912]{0:T(1024)(128)(4,1)}), s8[4194304]{0:T(1024)(128)(4,1)S(1)}, s32[]{:S(2)}) async-start(s8[12582912]{0:T(1024)(128)(4,1)} %bitcast.90), calls=%async_computation.10 | async-start | bytes 8388608
  383.4 7.1 %copy-start.12 = (bf16[512,768]{0,1:T(8,128)(2,1)S(1)}, bf16[512,768]{0,1:T(8,128)(2,1)}, u32[]{:S(2)}) copy-start(bf16[512,768]{0,1:T(8,128)(2,1)} %copy.58) | copy-start | bytes 2359300
  595.6 6.6 %copy-start.21 = (f32[768,768]{1,0:T(8,128)S(1)}, f32[768,768]{1,0:T(8,128)}, u32[]{:S(2)}) copy-start(f32[768,768]{1,0:T(8,128)} %get-tuple-element.75) | copy-start | bytes 7077892
  (24 other events, 77.3 us)
Sparse Core Ops, SparseCore 0:
  9.6 40.1 all-gather.2
  51.3 37.4 all-gather.4
  218.7 138.2 reduce-scatter.1
  404.2 191.3 all-reduce.3
